TPU v7x, 512 devices: a whole 4x8x8 slice. The times are simulated.
512 devices in a mesh: wide: 64 (over z, y_hi, core), narrow: 8 (over y_lo, x).
Axes of the slice: x: 4, y: 8 (y_hi: 4, y_lo: 2; y = y_hi * 2 + y_lo), z: 8, core: 2. Of those that a mesh axis runs over, the one named last changes fastest.
Arguments:
- tile_values: bfloat16 [3584, 512, 512], P(('wide', 'narrow')), may hold values from -0.25 to 0.25
- tile_row: int32 [3584], P(('wide', 'narrow')), may hold values from 0 to 1
- tile_col: int32 [3584], P(('wide', 'narrow')), may hold values from 0 to 7
- basis: float32 [524288, 256], P(('wide', 'narrow')), may hold values from -6 to 6
Outputs:
- next_basis: float32 [4096, 256], P('wide')
All inputs are finite; a program needn't handle non-finite values.
Results may differ from a plain program's by a relative error of at most 0.0032.
Values sent between devices are 32-bit elements; how exact they have to be, the bound alone decides.
No kernel may reach another device: no remote copies, remote signals or barrier semaphores. Data moves between devices by JAX's collectives and lax.ppermute only.
A program may use at most 64 MiB of HBM per device.

v0:
```python
import jax
import jax.numpy as jnp
from jax import lax
from jax.sharding import PartitionSpec as P

COLS_DEV = 64


def finish(owned_rows, gram_sum):
    factor = jnp.linalg.cholesky(gram_sum)
    return jax.scipy.linalg.solve_triangular(factor, owned_rows.T, lower=True).T


def gram_terms(owned_rows):
    return jnp.dot(
        owned_rows.T,
        owned_rows,
        precision=lax.Precision.HIGHEST,
        preferred_element_type=jnp.float32,
    )


def body(tile_values, tile_row, tile_col, basis):
    tile_edge = tile_values.shape[1]
    basis_width = basis.shape[1]
    blocks = basis.astype(jnp.bfloat16).reshape(basis.shape[0] // tile_edge, tile_edge, basis_width)
    chosen = jnp.take(blocks, tile_row, axis=0)
    products = jnp.einsum("tij,tik->tjk", tile_values, chosen, preferred_element_type=jnp.float32)
    col_blocks = COLS_DEV * lax.axis_size("wide") // tile_edge
    one_hot = (tile_col[None, :] == jnp.arange(col_blocks, dtype=jnp.int32)[:, None]).astype(
        jnp.float32
    )
    partial_value = jnp.einsum("ct,tjk->cjk", one_hot, products, precision=lax.Precision.HIGHEST)
    total_rows = col_blocks * tile_edge
    partial_value = partial_value.reshape(total_rows, basis_width)
    reduced = lax.psum_scatter(partial_value, "wide", scatter_dimension=0, tiled=True)
    owned_rows = lax.psum(reduced, "narrow")
    gram_sum = lax.psum(gram_terms(owned_rows), "wide") / total_rows
    return finish(owned_rows, gram_sum)


def solution(mesh):
    in_specs = (
        P(("wide", "narrow"), None, None),
        P(("wide", "narrow")),
        P(("wide", "narrow")),
        P(("wide", "narrow"), None),
    )
    out_specs = P("wide", None)
    return jax.shard_map(body, mesh=mesh, in_specs=in_specs, out_specs=out_specs, check_vma=False)
```

profile of v0, /device:TPU:1, one launch (start us, length us, event | category | flops | bytes accessed | tf_op | source)
XLA Modules:
  0.0 864.6 jit_solution(9576807460728252653)
XLA Ops:
  6.5 0.0 reduce-scatter.2.cloned.1.call-start
  6.5 0.7 compare_select_fusion
  7.2 0.7 compare_and_fusion
  7.9 1.3 convert_element_type.4
  9.2 0.7 gather_fusion
  9.8 5.1 fusion.2
  15.0 0.0 copy-start.1
  15.0 5.3 copy.10
  20.2 0.0 copy-done.1
  20.2 4.2 fusion
  24.5 3.2 copy.7
  27.7 0.0 reduce-scatter.2.cloned.1.call-update
  27.7 0.0 all-reduce.4.cloned.1.call-start
  27.7 157.9 %reduce-scatter.2.cloned.1.call-done = f32[64,256]{1,0:T(8,128)} async-done(((f32[4096,256]{1,0:T(8,128)}), f32[64,256]{1,0:T(8,128)}) %reduce-scatter.2.cloned.1.call-update) | async-done | bytes 65552 | tf_op jit(solution)/shard_map/reduce_scatter | solution.py:36
  185.6 0.0 all-reduce.4.cloned.1.call-update
  185.6 0.2 all-reduce.6.cloned.1.call-start
  185.9 83.3 %all-reduce.4.cloned.1.call-done = f32[64,256]{1,0:T(8,128)} async-done(((f32[64,256]{1,0:T(8,128)}), f32[64,256]{1,0:T(8,128)}) %all-reduce.4.cloned.1.call-update) | async-done | bytes 65552 | tf_op jit(solution)/shard_map/psum | solution.py:37
  269.2 0.0 copy-start
  269.2 2.1 fusion.19
  271.2 0.0 all-reduce.6.cloned.1.call-update
  271.3 523.6 %all-reduce.6.cloned.1.call-done = f32[256,256]{0,1:T(8,128)} async-done(((f32[256,256]{0,1:T(8,128)}), f32[256,256]{0,1:T(8,128)}) %all-reduce.6.cloned.1.call-update) | async-done | bytes 262160 | tf_op jit(solution)/shard_map/psum | solution.py:38
  794.8 1.0 broadcast_multiply_fusion
  795.8 0.1 copy.9
  796.0 1.0 fusion.6
  797.0 11.7 %cholesky.50 = f32[128,128]{1,0:T(8,128)S(1)} custom-call(f32[128,128]{1,0:T(8,128)S(1)} %cholesky.118), custom_call_target="Cholesky" | custom-call | tf_op jit(solution)/shard_map/jit(cholesky)/cholesky | solution.py:10
  808.7 9.8 %custom-call.15 = f32[1,128,128]{1,2,0:T(8,128)S(1)} custom-call(f32[1,128,128]{2,1,0:T(8,128)S(1)} %get-tuple-element.26), custom_call_target="InvertDiagBlocksLowerTriangular" | custom-call | tf_op jit(solution)/shard_map/jit(cholesky)/cholesky | solution.py:10
  818.5 0.2 constant_dynamic-update-slice_fusion.1
  818.8 0.3 convolution_subtract_fusion
  819.0 11.7 %cholesky.105 = f32[128,128]{1,0:T(8,128)S(1)} custom-call(f32[128,128]{1,0:T(8,128)S(1)} %convolution_subtract_fusion), custom_call_target="Cholesky" | custom-call | tf_op jit(solution)/shard_map/jit(cholesky)/cholesky | solution.py:10
  830.8 0.7 compare_reduce_fusion
  832.8 0.1 triangular_solve.57
  832.9 4.2 while.1
  833.1 0.7 fusion.28
  833.7 1.3 bitcast_dynamic-update-slice_fusion.2
  835.1 0.7 fusion.28
  835.8 1.3 bitcast_dynamic-update-slice_fusion.2
  837.1 19.7 %custom-call.16 = f32[2,128,128]{1,2,0:T(8,128)S(1)} custom-call(f32[2,128,128]{2,1,0:T(8,128)S(1)} %get-tuple-element.12), custom_call_target="InvertDiagBlocksLowerTriangular" | custom-call | tf_op jit(solution)/shard_map/jit(_solve_triangular)/triangular_solve | solution.py:11
  856.8 0.0 copy-done
  856.8 0.2 fusion.9
  857.0 0.2 convolution_subtract_fusion.1
  857.2 0.2 fusion.8
  857.4 0.6 maximum_bitcast_fusion
  (10 shorter events, 0.2 us)
Async XLA Ops:
  6.5 179.1 %reduce-scatter.2.cloned.1.call-start = ((), (), s32[]{:S(2)}) async-start(), calls=%async_computation.1 | async-start | bytes 4259840 | tf_op jit(solution)/shard_map/reduce_scatter | solution.py:36
  15.0 5.3 copy-start.1
  27.7 241.5 %all-reduce.4.cloned.1.call-start = ((), (), s32[]{:S(2)}) async-start(), calls=%async_computation.2 | async-start | bytes 131072 | tf_op jit(solution)/shard_map/psum | solution.py:37
  185.6 609.2 %all-reduce.6.cloned.1.call-start = ((), (), s32[]{:S(2)}) async-start(), calls=%async_computation.3 | async-start | bytes 524288 | tf_op jit(solution)/shard_map/psum | solution.py:38
  269.2 587.6 %copy-start = (f32[64,256]{1,0:T(8,128)S(1)}, f32[64,256]{1,0:T(8,128)}, u32[]{:S(2)}) copy-start(f32[64,256]{1,0:T(8,128)} %all-reduce.4.cloned.1.call-done) | copy-start | bytes 196612
Sparse Core Ops, SparseCore 0:
  27.8 157.7 reduce-scatter.1
  188.5 80.6 all-reduce.3
  272.1 522.7 all-reduce.5
where the time goes:
time: 865 us
  waiting for transfers between devices  765 us (88%)
  other arithmetic  58.9 us (7%)
  between operations  14.5 us (2%)
  local copies, waits for them, and re-layouts  13.4 us (2%)
  matrix products  12.5 us (1%)
    psum x1, waiting for transfers between devices, body(): gram_sum = lax.psum(gram_terms(owned_rows), 'wide') / total_rows  524 us
    reduce_scatter x1, waiting for transfers between devices, body(): lax.psum_scatter(partial_value, 'wide', scatter_dimension=0, tiled=True)  158 us
    psum x1, waiting for transfers between devices, body(): owned_rows = lax.psum(reduced, 'narrow')  83.3 us
    another operation x6, other arithmetic, finish(): factor = jnp.linalg.cholesky(gram_sum)  34 us
    another operation x3, other arithmetic, finish(): return jax.scipy.linalg.solve_triangular(factor, owned_rows.T, lower=True).T  19.7 us
  transfers between devices with their start and end apart: 3, of which 3 were waited for; matrix products, arithmetic and copies ran while one was open for 0% of the time, Pallas kernels for 0%

commit v1 on v0

--- a/solution.py
+++ b/solution.py
@@ -35,7 +35,7 @@
     partial_value = partial_value.reshape(total_rows, basis_width)
     reduced = lax.psum_scatter(partial_value, "wide", scatter_dimension=0, tiled=True)
     owned_rows = lax.psum(reduced, "narrow")
-    gram_sum = lax.psum(gram_terms(owned_rows), "wide") / total_rows
+    gram_sum = jnp.sum(lax.all_gather(gram_terms(owned_rows), "wide"), axis=0) / total_rows
     return finish(owned_rows, gram_sum)
 
 

time: 865 us -> 493 us (0.57)
  waiting for transfers between devices: 765 us -> 387 us
    psum x1 -> x0, waiting for transfers between devices: 524 us -> none  [body(): gram_sum = lax.psum(gram_terms(owned_rows), 'wide') / total_rows]
    all_gather x0 -> x1, waiting for transfers between devices: none -> 146 us  [body(): lax.all_gather(gram_terms(owned_rows), 'wide')]
where the time goes in v1:
time: 493 us; the launch traced here: 492 us
  waiting for transfers between devices  387 us (78%)
  other arithmetic  63.9 us (13%)
  between operations  14.5 us (3%)
  local copies, waits for them, and re-layouts  13.4 us (3%)
  matrix products  12.5 us (3%)
    reduce_scatter x1, waiting for transfers between devices, body(): lax.psum_scatter(partial_value, 'wide', scatter_dimension=0, tiled=True)  158 us
    all_gather x1, waiting for transfers between devices, body(): lax.all_gather(gram_terms(owned_rows), 'wide')  146 us
    psum x1, waiting for transfers between devices, body(): owned_rows = lax.psum(reduced, 'narrow')  83.3 us
    another operation x6, other arithmetic, finish(): factor = jnp.linalg.cholesky(gram_sum)  34 us
    another operation x3, other arithmetic, finish(): return jax.scipy.linalg.solve_triangular(factor, owned_rows.T, lower=True).T  19.7 us
  transfers between devices with their start and end apart: 3, of which 3 were waited for; matrix products, arithmetic and copies ran while one was open for 0% of the time, Pallas kernels for 0%

profile of v1, /device:TPU:1, one launch (start us, length us, event | category | flops | bytes accessed | tf_op | source)
XLA Modules:
  0.0 492.2 jit_solution(11907528115673163367)
XLA Ops:
  6.5 0.0 reduce-scatter.2.cloned.1.call-start
  6.5 0.7 compare_select_fusion
  7.2 0.7 compare_and_fusion
  7.9 1.3 convert_element_type.4
  9.2 0.7 gather_fusion
  9.8 5.1 %convolution_bitcast_fusion = f32[7,512,256]{1,2,0:T(8,128)} fusion(bf16[7,512,512]{2,1,0:T(8,128)(2,1)} %param.4, bf16[7,512,256]{2,1,0:T(8,128)(2,1)S(1)} %gather_fusion, pred[7]{0:T(512)(128)(4,1)S(1)} %compare_and_fusion), kind=kOutput, calls=%fused_computation.3 | convolution fusion | flops 940441600 | bytes 9175047 | tf_op jit(solution)/shard_map/tij,tik->tjk/dot_general | solution.py:28
  15.0 0.0 copy-start.1
  15.0 5.3 %copy.12 = f32[7,512,256]{2,0,1:T(8,128)} copy(f32[7,512,256]{1,2,0:T(8,128)} %convolution_bitcast_fusion) | data formatting | bytes 7340032 | tf_op jit(solution)/shard_map/tij,tik->tjk/dot_general | solution.py:28
  20.2 0.0 copy-done.1
  20.2 4.2 fusion.12
  24.5 3.2 copy.13
  27.7 0.0 reduce-scatter.2.cloned.1.call-update
  27.7 0.0 all-reduce.3.cloned.1.call-start
  27.7 157.9 %reduce-scatter.2.cloned.1.call-done = f32[64,256]{1,0:T(8,128)} async-done(((f32[4096,256]{1,0:T(8,128)}), f32[64,256]{1,0:T(8,128)}) %reduce-scatter.2.cloned.1.call-update) | async-done | bytes 65552 | tf_op jit(solution)/shard_map/reduce_scatter | solution.py:36
  185.6 0.0 all-reduce.3.cloned.1.call-update
  185.6 0.2 all-gather.3.cloned.1.call-start
  185.9 83.3 %all-reduce.3.cloned.1.call-done = f32[64,256]{1,0:T(8,128)} async-done(((f32[64,256]{1,0:T(8,128)}), f32[64,256]{1,0:T(8,128)}) %all-reduce.3.cloned.1.call-update) | async-done | bytes 65552 | tf_op jit(solution)/shard_map/psum | solution.py:37
  269.2 2.0 fusion.17
  271.2 0.0 all-gather.3.cloned.1.call-update
  271.2 146.2 %all-gather.3.cloned.1.call-done = f32[16384,256]{1,0:T(8,128)} async-done(((f32[256,256]{1,0:T(8,128)}), f32[16384,256]{1,0:T(8,128)}) %all-gather.3.cloned.1.call-update) | async-done | bytes 16777232 | tf_op jit(solution)/shard_map/all_gather | solution.py:38
  417.5 6.8 %reduce_sum.11 = f32[256,256]{1,0:T(8,128)S(1)} reduce(f32[64,256,256]{2,1,0:T(8,128)} %bitcast.46, f32[]{:T(128)} %constant.94.clone.1), dimensions={0}, to_apply=%region_2.3 | reduce | flops 4128768 | bytes 17039364 | tf_op jit(solution)/shard_map/reduce_sum | solution.py:38
  424.3 0.0 copy-start
  424.3 0.1 copy.14
  424.5 11.7 %cholesky.50 = f32[128,128]{1,0:T(8,128)S(1)} custom-call(f32[128,128]{1,0:T(8,128)S(1)} %cholesky.118), custom_call_target="Cholesky" | custom-call | tf_op jit(solution)/shard_map/jit(cholesky)/cholesky | solution.py:10
  436.3 9.8 %custom-call.15 = f32[1,128,128]{1,2,0:T(8,128)S(1)} custom-call(f32[1,128,128]{2,1,0:T(8,128)S(1)} %get-tuple-element.26), custom_call_target="InvertDiagBlocksLowerTriangular" | custom-call | tf_op jit(solution)/shard_map/jit(cholesky)/cholesky | solution.py:10
  446.1 0.2 constant_dynamic-update-slice_fusion.1
  446.3 0.3 convolution_subtract_fusion
  446.6 11.7 %cholesky.105 = f32[128,128]{1,0:T(8,128)S(1)} custom-call(f32[128,128]{1,0:T(8,128)S(1)} %convolution_subtract_fusion), custom_call_target="Cholesky" | custom-call | tf_op jit(solution)/shard_map/jit(cholesky)/cholesky | solution.py:10
  458.3 0.7 compare_reduce_fusion
  460.4 0.1 triangular_solve.57
  460.4 4.2 while.1
  460.6 0.7 fusion.27
  461.3 1.3 bitcast_dynamic-update-slice_fusion.2
  462.7 0.7 fusion.27
  463.3 1.3 bitcast_dynamic-update-slice_fusion.2
  464.7 19.7 %custom-call.16 = f32[2,128,128]{1,2,0:T(8,128)S(1)} custom-call(f32[2,128,128]{2,1,0:T(8,128)S(1)} %get-tuple-element.12), custom_call_target="InvertDiagBlocksLowerTriangular" | custom-call | tf_op jit(solution)/shard_map/jit(_solve_triangular)/triangular_solve | solution.py:11
  484.4 0.0 copy-done
  484.4 0.2 fusion.6
  484.6 0.2 convolution_subtract_fusion.1
  484.8 0.2 fusion.5
  485.0 0.6 maximum_bitcast_fusion
  (11 shorter events, 0.2 us)
Async XLA Ops:
  6.5 179.1 %reduce-scatter.2.cloned.1.call-start = ((), (), s32[]{:S(2)}) async-start(), calls=%async_computation.1 | async-start | bytes 4259840 | tf_op jit(solution)/shard_map/reduce_scatter | solution.py:36
  15.0 5.3 %copy-start.1 = (s32[7]{0:T(128)S(1)}, s32[7]{0:T(128)}, u32[]{:S(2)}) copy-start(s32[7]{0:T(128)} %param.6) | copy-start | bytes 88
  27.7 241.5 %all-reduce.3.cloned.1.call-start = ((), (), s32[]{:S(2)}) async-start(), calls=%async_computation.2 | async-start | bytes 131072 | tf_op jit(solution)/shard_map/psum | solution.py:37
  185.6 231.9 %all-gather.3.cloned.1.call-start = ((), (), s32[]{:S(2)}) async-start(), calls=%async_computation.3 | async-start | bytes 17039360 | tf_op jit(solution)/shard_map/all_gather | solution.py:38
  424.3 60.0 %copy-start = (f32[64,256]{1,0:T(8,128)S(1)}, f32[64,256]{1,0:T(8,128)}, u32[]{:S(2)}) copy-start(f32[64,256]{1,0:T(8,128)} %all-reduce.3.cloned.1.call-done) | copy-start | bytes 196612
Sparse Core Ops, SparseCore 0:
  27.8 157.7 reduce-scatter.1
  188.5 80.6 all-reduce.2
  272.5 144.9 all-gather.2
